TPU v7x, 32 devices: a whole 2x2x4 slice. The times are simulated.
32 devices in a mesh: gx: 4 (over y, core), gy: 8 (over z, x).
Axes of the slice: x: 2, y: 2, z: 4, core: 2. Of those that a mesh axis runs over, the one named last changes fastest.
Arguments:
- density: float32 [80, 80, 384], P('gx', 'gy'), may hold values from 1e-06 to 0.5
- charge: float32 [80, 80, 384], P('gx', 'gy'), may hold values from -6 to 6
Outputs:
- solution_field: float32 [80, 80, 384], P('gx', 'gy')
- residual: float32 [80, 80, 384], P('gx', 'gy')
All inputs are finite; a program needn't handle non-finite values.
Results may differ from a plain program's by a relative error of at most 0.0003.
Values sent between devices are 32-bit elements; how exact they have to be, the bound alone decides.
No kernel may reach another device: no remote copies, remote signals or barrier semaphores. Data moves between devices by JAX's collectives and lax.ppermute only.
A program may use at most 64 MiB of HBM per device.

v0:
```python
import math
import jax
import jax.numpy as jnp
from jax import lax
from jax.sharding import PartitionSpec as P

EPS_SOLVENT = 78.3
RHO_UPPER = 0.005
RHO_LOWER = 0.0001
KAPPA_SCALE = 0.1
EPS_PRECOND = 20.0
SHIFT_PRECOND = 0.05
HIGHEST = lax.Precision.HIGHEST


def extended(block, sides, width):
    for axis, dim in sides:
        count = lax.axis_size(axis)
        forward = [(i, i + 1) for i in range(count - 1)]
        forward.append((count - 1, 0))
        backward = [(target, source) for source, target in forward]
        low = lax.ppermute(
            lax.slice_in_dim(block, block.shape[dim] - width, None, axis=dim), axis, forward
        )
        high = lax.ppermute(lax.slice_in_dim(block, 0, width, axis=dim), axis, backward)
        block = jnp.concatenate([low, block, high], axis=dim)
    return block


def permittivity(density):
    upper = math.log(RHO_UPPER)
    lower = math.log(RHO_LOWER)
    fraction = jnp.clip((upper - jnp.log(density)) / (upper - lower), 0.0, 1.0)
    exponent = fraction - jnp.sin(2.0 * math.pi * fraction) / (2.0 * math.pi)
    return jnp.exp(exponent * math.log(EPS_SOLVENT))


def hartley(length):
    indices = jnp.arange(length, dtype=jnp.int32)
    product = indices[:, None] * indices[None, :] % length
    angles = product.astype(jnp.float32) * (2.0 * math.pi / length)
    return jnp.cos(angles) + jnp.sin(angles)


def spectrum(wavenum, length):
    halfang = wavenum.astype(jnp.float32) * (math.pi / length)
    return ((27.0 * jnp.sin(halfang) - jnp.sin(3.0 * halfang)) / 12.0) ** 2


def cutout(values, offset, length, dimen):
    return lax.slice_in_dim(values, offset, offset + length, axis=dimen)


def padded_term(padded, faces, count, dimen):
    nfaces = count + 3
    grad = (
        27.0 * (cutout(padded, 2, nfaces, dimen) - cutout(padded, 1, nfaces, dimen))
        - (cutout(padded, 3, nfaces, dimen) - cutout(padded, 0, nfaces, dimen))
    ) / 24.0
    flux = faces * grad
    return (
        27.0 * (cutout(flux, 2, count, dimen) - cutout(flux, 1, count, dimen))
        - (cutout(flux, 3, count, dimen) - cutout(flux, 0, count, dimen))
    ) / 24.0


def rolled_term(field, faces):
    grad = (
        27.0 * (jnp.roll(field, -1, 2) - field) - (jnp.roll(field, -2, 2) - jnp.roll(field, 1, 2))
    ) / 24.0
    flux = faces * grad
    return (
        27.0 * (flux - jnp.roll(flux, 1, 2)) - (jnp.roll(flux, -1, 2) - jnp.roll(flux, 2, 2))
    ) / 24.0


def operate(field, faces_x, faces_y, faces_z, kappa):
    cellsx = field.shape[0]
    cellsy = field.shape[1]
    padded = extended(field, (("gx", 0), ("gy", 1)), 3)
    term_x = padded_term(padded[:, 3 : 3 + cellsy], faces_x, cellsx, 0)
    term_y = padded_term(padded[3 : 3 + cellsx], faces_y, cellsy, 1)
    term_z = rolled_term(field, faces_z)
    return kappa * field - (term_x + term_y + term_z)


def precondition(field):
    cellsx, cellsy, length_z = field.shape
    size_x = cellsx * lax.axis_size("gx")
    size_y = cellsy * lax.axis_size("gy")
    hart_x = hartley(size_x)
    hart_y = hartley(size_y)
    hart_z = hartley(length_z)
    scaling = float(size_x * size_y * length_z)
    forward = jnp.dot(field, hart_z, precision=HIGHEST)
    zpiece = length_z // lax.axis_size("gx")
    xpiece = size_x // lax.axis_size("gy")
    lines_x = lax.all_to_all(forward, "gx", split_axis=2, concat_axis=0, tiled=True)
    along_x = jnp.einsum("xyk,xa->yka", lines_x, hart_x, precision=HIGHEST)
    lines_y = lax.all_to_all(along_x, "gy", split_axis=2, concat_axis=0, tiled=True)
    along_y = jnp.einsum("ykb,yc->kbc", lines_y, hart_y, precision=HIGHEST)
    wave_z = lax.axis_index("gx") * zpiece + jnp.arange(zpiece, dtype=jnp.int32)
    wave_x = lax.axis_index("gy") * xpiece + jnp.arange(xpiece, dtype=jnp.int32)
    wave_y = jnp.arange(size_y, dtype=jnp.int32)
    symbol = (
        EPS_PRECOND
        * (
            spectrum(wave_z, length_z)[:, None, None]
            + spectrum(wave_x, size_x)[None, :, None]
            + spectrum(wave_y, size_y)[None, None, :]
        )
        + SHIFT_PRECOND
    )
    scaled = along_y / (symbol * scaling)
    back_y = jnp.einsum("kbc,cy->ykb", scaled, hart_y, precision=HIGHEST)
    lines_back = lax.all_to_all(back_y, "gy", split_axis=0, concat_axis=2, tiled=True)
    back_x = jnp.einsum("yka,ax->xyk", lines_back, hart_x, precision=HIGHEST)
    bricks = lax.all_to_all(back_x, "gx", split_axis=0, concat_axis=2, tiled=True)
    return jnp.dot(bricks, hart_z, precision=HIGHEST)


def residual_inner(residual, precond):
    return lax.psum(jnp.sum(residual * precond), ("gx", "gy"))


def local(density, charge):
    eps = permittivity(density)
    kappa = KAPPA_SCALE * (eps - 1.0) / (EPS_SOLVENT - 1.0)
    cellsx = eps.shape[0]
    cellsy = eps.shape[1]
    eps_padded = extended(eps, (("gx", 0), ("gy", 1)), 2)
    strip_x = eps_padded[:, 2 : 2 + cellsy]
    faces_x = 0.5 * (strip_x[:-1] + strip_x[1:])
    strip_y = eps_padded[2 : 2 + cellsx]
    faces_y = 0.5 * (strip_y[:, :-1] + strip_y[:, 1:])
    faces_z = 0.5 * (eps + jnp.roll(eps, -1, 2))
    rhs = 4.0 * math.pi * charge
    residual = rhs
    precond = precondition(residual)
    inner_now = residual_inner(residual, precond)
    image = operate(precond, faces_x, faces_y, faces_z, kappa)
    alpha = inner_now / lax.psum(jnp.sum(precond * image), ("gx", "gy"))
    solution_field = alpha * precond
    residual = residual - alpha * image
    return (solution_field, residual)


def solution(mesh):
    placed = (P("gx", "gy", None), P("gx", "gy", None))
    return jax.shard_map(
        local,
        mesh=mesh,
        in_specs=placed,
        out_specs=(P("gx", "gy", None), P("gx", "gy", None)),
        check_vma=False,
    )
```

profile of v0, /device:TPU:12, one launch (start us, length us, event | category | flops | bytes accessed | tf_op | source)
XLA Modules:
  0.0 139.1 jit_solution(10146124797497846084)
XLA Ops:
  0.6 4.3 %fusion.4 = f32[20,10,384]{2,0,1:T(8,128)S(1)} fusion(f32[20,10,384]{2,0,1:T(8,128)} %param.3), kind=kOutput, calls=%fused_computation.7 | convolution fusion | flops 355445760 | bytes 614400 | tf_op jit(solution)/shard_map/dot_general | solution.py:95
  4.9 1.4 %copy.11 = f32[20,10,384]{0,1,2:T(8,128)S(1)} copy(f32[20,10,384]{2,0,1:T(8,128)S(1)} %fusion.4) | data formatting | bytes 614400 | tf_op jit(solution)/shard_map/dot_general | solution.py:95
  6.3 1.9 %reshape.76 = f32[4,1,19200]{2,1,0:T(1,128)} reshape(f32[384,10,20]{2,1,0:T(8,128)S(1)} %bitcast.54) | data formatting | bytes 614400
  8.2 3.9 %all-to-all-start = ((f32[4,1,19200]{2,1,0:T(1,128)}), f32[4,1,19200]{2,1,0:T(1,128)S(1)}, u32[]{:S(2)}, u32[]{:S(2)}) async-start(f32[4,1,19200]{2,1,0:T(1,128)} %reshape.76), calls=%async_computation | async-start | bytes 614400 | tf_op jit(solution)/shard_map/all_to_all | solution.py:98
  12.1 4.9 %all-to-all-done = f32[4,1,19200]{2,1,0:T(1,128)S(1)} async-done(((f32[4,1,19200]{2,1,0:T(1,128)}), f32[4,1,19200]{2,1,0:T(1,128)S(1)}, u32[]{:S(2)}, u32[]{:S(2)}) %all-to-all-start) | async-done | bytes 307232 | tf_op jit(solution)/shard_map/all_to_all | solution.py:98
  17.0 0.5 broadcast.171
  17.5 1.5 %reduce = f32[4,19200]{1,0:T(4,128)S(1)} reduce(f32[4,1,19200]{2,1,0:T(1,128)S(1)} %all-to-all-done, f32[]{:T(128)} %broadcast.171), dimensions={1}, to_apply=%all_to_all.52.reduce_sub_computation | reduce | bytes 614404 | tf_op jit(solution)/shard_map/all_to_all | solution.py:98
  19.0 1.2 reshape.77
  20.3 1.9 %copy.12 = f32[20,10,4,96]{3,0,2,1:T(8,128)} copy(f32[20,10,4,96]{0,1,3,2:T(8,128)S(1)} %bitcast.53) | data formatting | bytes 614400 | tf_op jit(solution)/shard_map/all_to_all | solution.py:98
  22.2 1.1 all_to_all.55
  23.2 0.7 fusion.50
  24.1 1.3 reshape.78
  25.4 6.3 %all-to-all-start.1 = ((f32[8,1,9600]{2,1,0:T(1,128)}), f32[8,1,9600]{2,1,0:T(1,128)S(1)}, u32[]{:S(2)}, u32[]{:S(2)}) async-start(f32[8,1,9600]{2,1,0:T(1,128)} %reshape.78), calls=%async_computation.1 | async-start | bytes 614400 | tf_op jit(solution)/shard_map/all_to_all | solution.py:100
  31.9 8.7 %all-to-all-done.1 = f32[8,1,9600]{2,1,0:T(1,128)S(1)} async-done(((f32[8,1,9600]{2,1,0:T(1,128)}), f32[8,1,9600]{2,1,0:T(1,128)S(1)}, u32[]{:S(2)}, u32[]{:S(2)}) %all-to-all-start.1) | async-done | bytes 307232 | tf_op jit(solution)/shard_map/all_to_all | solution.py:100
  40.6 1.4 reduce.1
  41.9 0.3 reshape.79
  42.3 0.7 convolution_divide_fusion
  43.0 0.7 fusion.47
  43.9 1.3 reshape.80
  45.1 4.6 %all-to-all-start.2 = ((f32[8,1,9600]{2,1,0:T(1,128)}), f32[8,1,9600]{2,1,0:T(1,128)S(1)}, u32[]{:S(2)}, u32[]{:S(2)}) async-start(f32[8,1,9600]{2,1,0:T(1,128)} %reshape.80), calls=%async_computation.2 | async-start | bytes 614400 | tf_op jit(solution)/shard_map/all_to_all | solution.py:116
  49.7 1.3 multiply_exponential_fusion
  51.2 1.7 %collective-permute-start.1 = (f32[2,10,384]{2,0,1:T(2,128)S(1)}, f32[2,10,384]{2,0,1:T(2,128)S(1)}, u32[]{:S(2)}, u32[]{:S(2)}) collective-permute-start(f32[2,10,384]{2,0,1:T(2,128)S(1)} %get-tuple-element.12), channel_id=1, source_target_pairs={{8,0},{16,8},{24,16},{0,24},{9,1},{17,9},{25,17},{1,25},{10,2},{18... | collective-permute-start | bytes 92168 | tf_op jit(solution)/shard_map/ppermute | solution.py:25
  53.1 1.4 %collective-permute-done = f32[2,10,384]{2,0,1:T(2,128)S(1)} collective-permute-done((f32[2,10,384]{2,0,1:T(2,128)S(1)}, f32[2,10,384]{2,0,1:T(2,128)S(1)}, u32[]{:S(2)}, u32[]{:S(2)}) %collective-permute-start) | collective-permute-done | bytes 30752 | tf_op jit(solution)/shard_map/ppermute | solution.py:22
  54.5 1.5 %collective-permute-start.4 = (f32[24,2,384]{2,0,1:T(8,128)S(1)}, f32[24,2,384]{2,0,1:T(8,128)S(1)}, u32[]{:S(2)}, u32[]{:S(2)}) collective-permute-start(f32[24,2,384]{2,0,1:T(8,128)S(1)} %get-tuple-element.9), channel_id=1, source_target_pairs={{0,1},{1,2},{2,3},{3,4},{4,5},{5,6},{6,7},{7,0},{8,9},{9,10},{10,1... | collective-permute-start | bytes 221192 | tf_op jit(solution)/shard_map/ppermute | solution.py:22
  56.0 1.5 %collective-permute-start.5 = (f32[24,2,384]{2,0,1:T(8,128)S(1)}, f32[24,2,384]{2,0,1:T(8,128)S(1)}, u32[]{:S(2)}, u32[]{:S(2)}) collective-permute-start(f32[24,2,384]{2,0,1:T(8,128)S(1)} %get-tuple-element.10), channel_id=1, source_target_pairs={{1,0},{2,1},{3,2},{4,3},{5,4},{6,5},{7,6},{0,7},{9,8},{10,9},{11,1... | collective-permute-start | bytes 221192 | tf_op jit(solution)/shard_map/ppermute | solution.py:25
  57.5 0.7 all-to-all-done.2
  58.2 1.4 reduce.2
  59.6 0.3 reshape.81
  60.0 0.7 fusion.45
  60.9 1.3 reshape.82
  62.1 4.8 %all-to-all-start.3 = ((f32[4,1,19200]{2,1,0:T(1,128)}), f32[4,1,19200]{2,1,0:T(1,128)S(1)}, u32[]{:S(2)}, u32[]{:S(2)}) async-start(f32[4,1,19200]{2,1,0:T(1,128)} %reshape.82), calls=%async_computation.3 | async-start | bytes 614400 | tf_op jit(solution)/shard_map/all_to_all | solution.py:118
  67.1 4.7 %all-to-all-done.3 = f32[4,1,19200]{2,1,0:T(1,128)S(1)} async-done(((f32[4,1,19200]{2,1,0:T(1,128)}), f32[4,1,19200]{2,1,0:T(1,128)S(1)}, u32[]{:S(2)}, u32[]{:S(2)}) %all-to-all-start.3) | async-done | bytes 307232 | tf_op jit(solution)/shard_map/all_to_all | solution.py:118
  71.8 1.5 %reduce.3 = f32[4,19200]{1,0:T(4,128)S(1)} reduce(f32[4,1,19200]{2,1,0:T(1,128)S(1)} %all-to-all-done.3, f32[]{:T(128)} %broadcast.171), dimensions={1}, to_apply=%all_to_all.64.reduce_sub_computation | reduce | bytes 614404 | tf_op jit(solution)/shard_map/all_to_all | solution.py:118
  73.3 0.3 reshape.83
  73.6 0.3 copy.21
  73.9 0.2 all_to_all.67
  74.2 3.3 %fusion.2 = f32[20,10,384]{2,0,1:T(8,128)S(1)} fusion(f32[20,10,384]{2,0,1:T(8,128)S(1)} %all_to_all.67), kind=kOutput, calls=%fused_computation.5 | convolution fusion | flops 355368960 | bytes 614400 | tf_op jit(solution)/shard_map/dot_general | solution.py:119
  78.0 1.7 %collective-permute-start.3 = (f32[3,10,384]{2,0,1:T(4,128)S(1)}, f32[3,10,384]{2,0,1:T(4,128)S(1)}, u32[]{:S(2)}, u32[]{:S(2)}) collective-permute-start(f32[3,10,384]{2,0,1:T(4,128)S(1)} %get-tuple-element.14), channel_id=1, source_target_pairs={{8,0},{16,8},{24,16},{0,24},{9,1},{17,9},{25,17},{1,25},{10,2},{18... | collective-permute-start | bytes 138248 | tf_op jit(solution)/shard_map/ppermute | solution.py:25
  79.7 1.5 %fusion.29 = f32[20,10,384]{2,0,1:T(8,128)S(1)} fusion(f32[20,10,1]{2,0,1:T(8,128)S(1)} %slice-done, f32[20,10,383]{2,0,1:T(8,128)S(1)} %slice.204, f32[20,10,384]{2,0,1:T(8,128)S(1)} %fusion.2, f32[20,10,1]{2,0,1:T(8,128)S(1)} %get-tuple-element.20, f32[20,10,383]{2,0,1:T(8,128)S(1)} %get-tuple-element.22, f32[20,10,2]{2,0,1:T(8,128)S(1)} %slice.209, ...), kind=kLoop, calls=%fused_computation.53 | loop fusion | flops 1459200 | bytes 2150400 | tf_op jit(solution)/shard_map/mul | solution.py:71
  81.8 0.2 collective-permute-start.6
  82.0 2.7 %collective-permute-start.7 = (f32[26,3,384]{2,0,1:T(8,128)S(1)}, f32[26,3,384]{2,0,1:T(8,128)S(1)}, u32[]{:S(2)}, u32[]{:S(2)}) collective-permute-start(f32[26,3,384]{2,0,1:T(8,128)S(1)} %get-tuple-element.7), channel_id=1, source_target_pairs={{1,0},{2,1},{3,2},{4,3},{5,4},{6,5},{7,6},{0,7},{9,8},{10,9},{11,1... | collective-permute-start | bytes 359432 | tf_op jit(solution)/shard_map/ppermute | solution.py:25
  84.7 0.2 fusion.26
  85.0 3.8 %collective-permute-done.6 = f32[26,3,384]{2,0,1:T(8,128)S(1)} collective-permute-done((f32[26,3,384]{2,0,1:T(8,128)S(1)}, f32[26,3,384]{2,0,1:T(8,128)S(1)}, u32[]{:S(2)}, u32[]{:S(2)}) %collective-permute-start.6) | collective-permute-done | bytes 119840 | tf_op jit(solution)/shard_map/ppermute | solution.py:22
  88.8 2.7 %collective-permute-done.7 = f32[26,3,384]{2,0,1:T(8,128)S(1)} collective-permute-done((f32[26,3,384]{2,0,1:T(8,128)S(1)}, f32[26,3,384]{2,0,1:T(8,128)S(1)}, u32[]{:S(2)}, u32[]{:S(2)}) %collective-permute-start.7) | collective-permute-done | bytes 119840 | tf_op jit(solution)/shard_map/ppermute | solution.py:25
  91.6 0.3 fusion.12
  91.9 2.5 %multiply_reduce_fusion = (f32[]{:T(128)}, f32[]{:T(128)}, f32[20,10,384]{2,0,1:T(8,128)S(1)}) fusion(f32[20,10,384]{2,0,1:T(8,128)S(1)} %fusion.2, f32[20,10,384]{2,0,1:T(8,128)S(1)} %copy-done.2, f32[20,10,382]{2,0,1:T(8,128)S(1)} %bitcast.52, f32[20,10,2]{2,0,1:T(8,128)S(1)} %slice.216, f32[20,10,1]{2,0,1:T(8,128)S(1)} %get-tuple-element.16, ...), kind=kLoop, calls=%fused_computation.64 | loop fusion | flops 2611198 | bytes 4915208 | tf_op jit(solution)/shard_map/reduce_sum | solution.py:142
  94.5 42.4 %all-reduce = (f32[]{:T(128)}, f32[]{:T(128)}) all-reduce(f32[]{:T(128)} %get-tuple-element.3, f32[]{:T(128)} %get-tuple-element.2), channel_id=1, replica_groups=mesh['gx'=4,'gy'=8] {'gx','gy'}, use_global_device_ids=true, to_apply=%region_1.2 | all-reduce | flops 2 | bytes 16 | tf_op jit(solution)/shard_map/psum | solution.py:123
  138.1 0.9 multiply_subtract_fusion
  (42 shorter events, 2.4 us)
Async XLA Ops:
  8.2 8.8 %all-to-all-start = ((f32[4,1,19200]{2,1,0:T(1,128)}), f32[4,1,19200]{2,1,0:T(1,128)S(1)}, u32[]{:S(2)}, u32[]{:S(2)}) async-start(f32[4,1,19200]{2,1,0:T(1,128)} %reshape.76), calls=%async_computation | async-start | bytes 614400 | tf_op jit(solution)/shard_map/all_to_all | solution.py:98
  25.4 15.2 %all-to-all-start.1 = ((f32[8,1,9600]{2,1,0:T(1,128)}), f32[8,1,9600]{2,1,0:T(1,128)S(1)}, u32[]{:S(2)}, u32[]{:S(2)}) async-start(f32[8,1,9600]{2,1,0:T(1,128)} %reshape.78), calls=%async_computation.1 | async-start | bytes 614400 | tf_op jit(solution)/shard_map/all_to_all | solution.py:100
  42.3 7.5 %copy-start.1 = (f32[20,10,384]{2,0,1:T(8,128)S(1)}, f32[20,10,384]{2,0,1:T(8,128)}, u32[]{:S(2)}) copy-start(f32[20,10,384]{2,0,1:T(8,128)} %param.2) | copy-start | bytes 921604
  45.1 13.1 %all-to-all-start.2 = ((f32[8,1,9600]{2,1,0:T(1,128)}), f32[8,1,9600]{2,1,0:T(1,128)S(1)}, u32[]{:S(2)}, u32[]{:S(2)}) async-start(f32[8,1,9600]{2,1,0:T(1,128)} %reshape.80), calls=%async_computation.2 | async-start | bytes 614400 | tf_op jit(solution)/shard_map/all_to_all | solution.py:116
  51.1 16.0 %copy-start = (f32[20,10,384]{2,0,1:T(8,128)}, f32[20,10,384]{2,0,1:T(8,128)S(1)}, u32[]{:S(2)}) copy-start(f32[20,10,384]{2,0,1:T(8,128)S(1)} %multiply_exponential_fusion) | copy-start | bytes 921604
  51.1 3.4 %collective-permute-start = (f32[2,10,384]{2,0,1:T(2,128)S(1)}, f32[2,10,384]{2,0,1:T(2,128)S(1)}, u32[]{:S(2)}, u32[]{:S(2)}) collective-permute-start(f32[2,10,384]{2,0,1:T(2,128)S(1)} %get-tuple-element.11), channel_id=1, source_target_pairs={{0,8},{8,16},{16,24},{24,0},{1,9},{9,17},{17,25},{25,1},{2,10},{10... | collective-permute-start | bytes 92168 | tf_op jit(solution)/shard_map/ppermute | solution.py:22
  51.2 3.3 %collective-permute-start.1 = (f32[2,10,384]{2,0,1:T(2,128)S(1)}, f32[2,10,384]{2,0,1:T(2,128)S(1)}, u32[]{:S(2)}, u32[]{:S(2)}) collective-permute-start(f32[2,10,384]{2,0,1:T(2,128)S(1)} %get-tuple-element.12), channel_id=1, source_target_pairs={{8,0},{16,8},{24,16},{0,24},{9,1},{17,9},{25,17},{1,25},{10,2},{18... | collective-permute-start | bytes 92168 | tf_op jit(solution)/shard_map/ppermute | solution.py:25
  54.5 12.5 %collective-permute-start.4 = (f32[24,2,384]{2,0,1:T(8,128)S(1)}, f32[24,2,384]{2,0,1:T(8,128)S(1)}, u32[]{:S(2)}, u32[]{:S(2)}) collective-permute-start(f32[24,2,384]{2,0,1:T(8,128)S(1)} %get-tuple-element.9), channel_id=1, source_target_pairs={{0,1},{1,2},{2,3},{3,4},{4,5},{5,6},{6,7},{7,0},{8,9},{9,10},{10,1... | collective-permute-start | bytes 221192 | tf_op jit(solution)/shard_map/ppermute | solution.py:22
  56.0 11.0 %collective-permute-start.5 = (f32[24,2,384]{2,0,1:T(8,128)S(1)}, f32[24,2,384]{2,0,1:T(8,128)S(1)}, u32[]{:S(2)}, u32[]{:S(2)}) collective-permute-start(f32[24,2,384]{2,0,1:T(8,128)S(1)} %get-tuple-element.10), channel_id=1, source_target_pairs={{1,0},{2,1},{3,2},{4,3},{5,4},{6,5},{7,6},{0,7},{9,8},{10,9},{11,1... | collective-permute-start | bytes 221192 | tf_op jit(solution)/shard_map/ppermute | solution.py:25
  62.1 9.7 %all-to-all-start.3 = ((f32[4,1,19200]{2,1,0:T(1,128)}), f32[4,1,19200]{2,1,0:T(1,128)S(1)}, u32[]{:S(2)}, u32[]{:S(2)}) async-start(f32[4,1,19200]{2,1,0:T(1,128)} %reshape.82), calls=%async_computation.3 | async-start | bytes 614400 | tf_op jit(solution)/shard_map/all_to_all | solution.py:118
  73.9 5.8 %slice-start = ((f32[20,10,384]{2,0,1:T(8,128)}), f32[20,10,1]{2,0,1:T(8,128)S(1)}, s32[]{:S(2)}) async-start(f32[20,10,384]{2,0,1:T(8,128)} %copy-done), calls=%async_computation.4 | async-start | bytes 245760 | tf_op jit(solution)/shard_map/jit(_roll_static)/slice | solution.py:136
  77.9 3.7 %collective-permute-start.2 = (f32[3,10,384]{2,0,1:T(4,128)S(1)}, f32[3,10,384]{2,0,1:T(4,128)S(1)}, u32[]{:S(2)}, u32[]{:S(2)}) collective-permute-start(f32[3,10,384]{2,0,1:T(4,128)S(1)} %get-tuple-element.13), channel_id=1, source_target_pairs={{0,8},{8,16},{16,24},{24,0},{1,9},{9,17},{17,25},{25,1},{2,10},{10... | collective-permute-start | bytes 138248 | tf_op jit(solution)/shard_map/ppermute | solution.py:22
  78.0 3.7 %collective-permute-start.3 = (f32[3,10,384]{2,0,1:T(4,128)S(1)}, f32[3,10,384]{2,0,1:T(4,128)S(1)}, u32[]{:S(2)}, u32[]{:S(2)}) collective-permute-start(f32[3,10,384]{2,0,1:T(4,128)S(1)} %get-tuple-element.14), channel_id=1, source_target_pairs={{8,0},{16,8},{24,16},{0,24},{9,1},{17,9},{25,17},{1,25},{10,2},{18... | collective-permute-start | bytes 138248 | tf_op jit(solution)/shard_map/ppermute | solution.py:25
  81.8 7.0 %collective-permute-start.6 = (f32[26,3,384]{2,0,1:T(8,128)S(1)}, f32[26,3,384]{2,0,1:T(8,128)S(1)}, u32[]{:S(2)}, u32[]{:S(2)}) collective-permute-start(f32[26,3,384]{2,0,1:T(8,128)S(1)} %get-tuple-element.8), channel_id=1, source_target_pairs={{0,1},{1,2},{2,3},{3,4},{4,5},{5,6},{6,7},{7,0},{8,9},{9,10},{10,1... | collective-permute-start | bytes 359432 | tf_op jit(solution)/shard_map/ppermute | solution.py:22
  82.0 9.9 %copy-start.2 = (f32[20,10,384]{2,0,1:T(8,128)S(1)}, f32[20,10,384]{2,0,1:T(8,128)}, u32[]{:S(2)}) copy-start(f32[20,10,384]{2,0,1:T(8,128)} %param.3) | copy-start | bytes 921604
  82.0 9.5 %collective-permute-start.7 = (f32[26,3,384]{2,0,1:T(8,128)S(1)}, f32[26,3,384]{2,0,1:T(8,128)S(1)}, u32[]{:S(2)}, u32[]{:S(2)}) collective-permute-start(f32[26,3,384]{2,0,1:T(8,128)S(1)} %get-tuple-element.7), channel_id=1, source_target_pairs={{1,0},{2,1},{3,2},{4,3},{5,4},{6,5},{7,6},{0,7},{9,8},{10,9},{11,1... | collective-permute-start | bytes 359432 | tf_op jit(solution)/shard_map/ppermute | solution.py:25
where the time goes:
time: 140 us; the launch traced here: 139 us
  blocking collectives  42.4 us (30%)
  starting transfers between devices  29.1 us (21%)
  waiting for transfers between devices  26.9 us (19%)
  local copies, waits for them, and re-layouts  14.9 us (11%)
  other arithmetic  13.1 us (9%)
  matrix products  10.3 us (7%)
  between operations  2.36 us (2%)
    psum x1, blocking collectives, residual_inner(): return lax.psum(jnp.sum(residual * precond), ('gx', 'gy'))  42.4 us
    all_to_all x1, waiting for transfers between devices, precondition(): lax.all_to_all(along_x, 'gy', split_axis=2, concat_axis=0, tiled=True)  8.69 us
    unnamed x14, local copies, waits for them, and re-layouts  7.8 us
    ppermute x4, starting transfers between devices, extended(): lax.ppermute(lax.slice_in_dim(block, 0, width, axis=dim), axis, backward)  7.67 us
    all_to_all x1, starting transfers between devices, precondition(): lax.all_to_all(along_x, 'gy', split_axis=2, concat_axis=0, tiled=True)  6.25 us
    ppermute x4, waiting for transfers between devices, extended(): lax.ppermute(lax.slice_in_dim(block, block.shape[dim] - width, None, axis...  5.22 us
    all_to_all x1, waiting for transfers between devices, precondition(): lax.all_to_all(forward, 'gx', split_axis=2, concat_axis=0, tiled=True)  4.86 us
    all_to_all x1, starting transfers between devices, precondition(): lax.all_to_all(back_x, 'gx', split_axis=0, concat_axis=2, tiled=True)  4.82 us
  transfers between devices with their start and end apart: 12, of which 7 were waited for; matrix products, arithmetic and copies ran while one was open for 6% of the time, Pallas kernels for 0%

commit v1 on v0

--- a/solution.py
+++ b/solution.py
@@ -95,7 +95,12 @@
     forward = jnp.dot(field, hart_z, precision=HIGHEST)
     zpiece = length_z // lax.axis_size("gx")
     xpiece = size_x // lax.axis_size("gy")
-    lines_x = lax.all_to_all(forward, "gx", split_axis=2, concat_axis=0, tiled=True)
+    lines_x = jnp.concatenate(
+        jax.lax.all_to_all(
+            jnp.stack(jnp.split(forward, jax.lax.axis_size("gx"), axis=2), axis=0), "gx", 0, 0
+        ),
+        axis=0,
+    )
     along_x = jnp.einsum("xyk,xa->yka", lines_x, hart_x, precision=HIGHEST)
     lines_y = lax.all_to_all(along_x, "gy", split_axis=2, concat_axis=0, tiled=True)
     along_y = jnp.einsum("ykb,yc->kbc", lines_y, hart_y, precision=HIGHEST)

time: 140 us -> 134 us (0.957)
  local copies, waits for them, and re-layouts: 14.9 us -> 8.36 us
  waiting for transfers between devices: 26.9 us -> 28.7 us
    all_to_all x3 -> x1, local copies, waits for them, and re-layouts: 3.52 us -> 0.04 us  [precondition(): jax.lax.all_to_all(jnp.stack(jnp.split(forward, jax.lax.axis_size('gx'),...]
    unnamed x14 -> x12, local copies, waits for them, and re-layouts: 7.8 us -> 5.41 us
    all_to_all x1, waiting for transfers between devices: 4.86 us -> 6.83 us  [precondition(): jax.lax.all_to_all(jnp.stack(jnp.split(forward, jax.lax.axis_size('gx'),...]
    all_to_all x1 -> x0, other arithmetic: 1.49 us -> none  [precondition(): lax.all_to_all(forward, 'gx', split_axis=2, concat_axis=0, tiled=True)]
    dot_general x1 -> x0, local copies, waits for them, and re-layouts: 1.42 us -> none  [precondition(): forward = jnp.dot(field, hart_z, precision=HIGHEST)]
where the time goes in v1:
time: 134 us
  blocking collectives  42.5 us (32%)
  starting transfers between devices  29.3 us (22%)
  waiting for transfers between devices  28.7 us (21%)
  other arithmetic  12.4 us (9%)
  matrix products  10.3 us (8%)
  local copies, waits for them, and re-layouts  8.36 us (6%)
  between operations  2.35 us (2%)
    psum x1, blocking collectives, residual_inner(): return lax.psum(jnp.sum(residual * precond), ('gx', 'gy'))  42.5 us
    all_to_all x1, waiting for transfers between devices, precondition(): lax.all_to_all(along_x, 'gy', split_axis=2, concat_axis=0, tiled=True)  8.69 us
    ppermute x4, starting transfers between devices, extended(): lax.ppermute(lax.slice_in_dim(block, 0, width, axis=dim), axis, backward)  7.67 us
    all_to_all x1, waiting for transfers between devices, precondition(): jax.lax.all_to_all(jnp.stack(jnp.split(forward, jax.lax.axis_size('gx'),...  6.83 us
    all_to_all x1, starting transfers between devices, precondition(): lax.all_to_all(along_x, 'gy', split_axis=2, concat_axis=0, tiled=True)  6.25 us
    unnamed x12, local copies, waits for them, and re-layouts  5.41 us
    ppermute x4, waiting for transfers between devices, extended(): lax.ppermute(lax.slice_in_dim(block, block.shape[dim] - width, None, axis...  5.22 us
    all_to_all x1, starting transfers between devices, precondition(): lax.all_to_all(back_x, 'gx', split_axis=0, concat_axis=2, tiled=True)  4.82 us
  transfers between devices with their start and end apart: 12, of which 7 were waited for; matrix products, arithmetic and copies ran while one was open for 6% of the time, Pallas kernels for 0%

profile of v1, /device:TPU:12, one launch (start us, length us, event | category | flops | bytes accessed | tf_op | source)
XLA Modules:
  0.0 133.9 jit_solution(2906068588231922249)
XLA Ops:
  0.6 4.3 %fusion.4 = f32[20,10,384]{2,0,1:T(8,128)S(1)} fusion(f32[20,10,384]{2,0,1:T(8,128)} %param.3), kind=kOutput, calls=%fused_computation.7 | convolution fusion | flops 355445760 | bytes 614400 | tf_op jit(solution)/shard_map/dot_general | solution.py:95
  4.9 0.2 slice_bitcast_fusion.3
  5.1 0.8 pad_maximum_fusion.2
  5.9 3.9 %all-to-all-start = ((f32[4,20,10,96]{3,1,2,0:T(8,128)}), f32[4,20,10,96]{3,1,2,0:T(8,128)S(1)}, u32[]{:S(2)}, u32[]{:S(2)}) async-start(f32[4,20,10,96]{3,1,2,0:T(8,128)} %pad_maximum_fusion.2), calls=%async_computation | async-start | bytes 983040 | tf_op jit(solution)/shard_map/all_to_all | solution.py:99
  9.8 6.8 %all-to-all-done = f32[4,20,10,96]{3,1,2,0:T(8,128)S(1)} async-done(((f32[4,20,10,96]{3,1,2,0:T(8,128)}), f32[4,20,10,96]{3,1,2,0:T(8,128)S(1)}, u32[]{:S(2)}, u32[]{:S(2)}) %all-to-all-start) | async-done | bytes 307232 | tf_op jit(solution)/shard_map/all_to_all | solution.py:99
  16.7 0.7 fusion.50
  17.6 1.3 reshape.80
  18.9 6.3 %all-to-all-start.1 = ((f32[8,1,9600]{2,1,0:T(1,128)}), f32[8,1,9600]{2,1,0:T(1,128)S(1)}, u32[]{:S(2)}, u32[]{:S(2)}) async-start(f32[8,1,9600]{2,1,0:T(1,128)} %reshape.80), calls=%async_computation.1 | async-start | bytes 614400 | tf_op jit(solution)/shard_map/all_to_all | solution.py:105
  25.4 8.7 %all-to-all-done.1 = f32[8,1,9600]{2,1,0:T(1,128)S(1)} async-done(((f32[8,1,9600]{2,1,0:T(1,128)}), f32[8,1,9600]{2,1,0:T(1,128)S(1)}, u32[]{:S(2)}, u32[]{:S(2)}) %all-to-all-start.1) | async-done | bytes 307232 | tf_op jit(solution)/shard_map/all_to_all | solution.py:105
  34.1 0.6 broadcast.171
  34.6 1.3 %reduce = f32[8,9600]{1,0:T(8,128)S(1)} reduce(f32[8,1,9600]{2,1,0:T(1,128)S(1)} %all-to-all-done.1, f32[]{:T(128)} %broadcast.171), dimensions={1}, to_apply=%all_to_all.43.reduce_sub_computation | reduce | bytes 614404 | tf_op jit(solution)/shard_map/all_to_all | solution.py:105
  36.0 0.3 reshape.81
  36.4 0.7 convolution_divide_fusion
  37.1 0.7 fusion.47
  37.9 1.3 reshape.82
  39.2 4.7 %all-to-all-start.2 = ((f32[8,1,9600]{2,1,0:T(1,128)}), f32[8,1,9600]{2,1,0:T(1,128)S(1)}, u32[]{:S(2)}, u32[]{:S(2)}) async-start(f32[8,1,9600]{2,1,0:T(1,128)} %reshape.82), calls=%async_computation.2 | async-start | bytes 614400 | tf_op jit(solution)/shard_map/all_to_all | solution.py:121
  43.9 1.3 multiply_exponential_fusion
  45.4 1.7 %collective-permute-start.1 = (f32[2,10,384]{2,0,1:T(2,128)S(1)}, f32[2,10,384]{2,0,1:T(2,128)S(1)}, u32[]{:S(2)}, u32[]{:S(2)}) collective-permute-start(f32[2,10,384]{2,0,1:T(2,128)S(1)} %get-tuple-element.12), channel_id=1, source_target_pairs={{8,0},{16,8},{24,16},{0,24},{9,1},{17,9},{25,17},{1,25},{10,2},{18... | collective-permute-start | bytes 92168 | tf_op jit(solution)/shard_map/ppermute | solution.py:25
  47.3 1.4 %collective-permute-done = f32[2,10,384]{2,0,1:T(2,128)S(1)} collective-permute-done((f32[2,10,384]{2,0,1:T(2,128)S(1)}, f32[2,10,384]{2,0,1:T(2,128)S(1)}, u32[]{:S(2)}, u32[]{:S(2)}) %collective-permute-start) | collective-permute-done | bytes 30752 | tf_op jit(solution)/shard_map/ppermute | solution.py:22
  48.7 1.5 %collective-permute-start.4 = (f32[24,2,384]{2,0,1:T(8,128)S(1)}, f32[24,2,384]{2,0,1:T(8,128)S(1)}, u32[]{:S(2)}, u32[]{:S(2)}) collective-permute-start(f32[24,2,384]{2,0,1:T(8,128)S(1)} %get-tuple-element.9), channel_id=1, source_target_pairs={{0,1},{1,2},{2,3},{3,4},{4,5},{5,6},{6,7},{7,0},{8,9},{9,10},{10,1... | collective-permute-start | bytes 221192 | tf_op jit(solution)/shard_map/ppermute | solution.py:22
  50.2 1.5 %collective-permute-start.5 = (f32[24,2,384]{2,0,1:T(8,128)S(1)}, f32[24,2,384]{2,0,1:T(8,128)S(1)}, u32[]{:S(2)}, u32[]{:S(2)}) collective-permute-start(f32[24,2,384]{2,0,1:T(8,128)S(1)} %get-tuple-element.10), channel_id=1, source_target_pairs={{1,0},{2,1},{3,2},{4,3},{5,4},{6,5},{7,6},{0,7},{9,8},{10,9},{11,1... | collective-permute-start | bytes 221192 | tf_op jit(solution)/shard_map/ppermute | solution.py:25
  51.7 0.7 all-to-all-done.2
  52.4 1.4 %reduce.1 = f32[8,9600]{1,0:T(8,128)S(1)} reduce(f32[8,1,9600]{2,1,0:T(1,128)S(1)} %all-to-all-done.2, f32[]{:T(128)} %broadcast.171), dimensions={1}, to_apply=%all_to_all.47.reduce_sub_computation | reduce | bytes 614404 | tf_op jit(solution)/shard_map/all_to_all | solution.py:121
  53.8 0.3 reshape.83
  54.2 0.7 fusion.45
  55.0 1.3 reshape.84
  56.3 4.8 %all-to-all-start.3 = ((f32[4,1,19200]{2,1,0:T(1,128)}), f32[4,1,19200]{2,1,0:T(1,128)S(1)}, u32[]{:S(2)}, u32[]{:S(2)}) async-start(f32[4,1,19200]{2,1,0:T(1,128)} %reshape.84), calls=%async_computation.3 | async-start | bytes 614400 | tf_op jit(solution)/shard_map/all_to_all | solution.py:123
  61.3 4.7 %all-to-all-done.3 = f32[4,1,19200]{2,1,0:T(1,128)S(1)} async-done(((f32[4,1,19200]{2,1,0:T(1,128)}), f32[4,1,19200]{2,1,0:T(1,128)S(1)}, u32[]{:S(2)}, u32[]{:S(2)}) %all-to-all-start.3) | async-done | bytes 307232 | tf_op jit(solution)/shard_map/all_to_all | solution.py:123
  66.0 1.5 %reduce.2 = f32[4,19200]{1,0:T(4,128)S(1)} reduce(f32[4,1,19200]{2,1,0:T(1,128)S(1)} %all-to-all-done.3, f32[]{:T(128)} %broadcast.171), dimensions={1}, to_apply=%all_to_all.51.reduce_sub_computation | reduce | bytes 614404 | tf_op jit(solution)/shard_map/all_to_all | solution.py:123
  67.5 0.3 reshape.85
  67.8 0.3 copy.19
  68.1 0.2 all_to_all.54
  68.3 3.3 %fusion.2 = f32[20,10,384]{2,0,1:T(8,128)S(1)} fusion(f32[20,10,384]{2,0,1:T(8,128)S(1)} %all_to_all.54), kind=kOutput, calls=%fused_computation.5 | convolution fusion | flops 355368960 | bytes 614400 | tf_op jit(solution)/shard_map/dot_general | solution.py:124
  71.6 0.2 fusion.81
  71.9 0.2 slice.208
  72.1 1.7 %collective-permute-start.3 = (f32[3,10,384]{2,0,1:T(4,128)S(1)}, f32[3,10,384]{2,0,1:T(4,128)S(1)}, u32[]{:S(2)}, u32[]{:S(2)}) collective-permute-start(f32[3,10,384]{2,0,1:T(4,128)S(1)} %get-tuple-element.14), channel_id=1, source_target_pairs={{8,0},{16,8},{24,16},{0,24},{9,1},{17,9},{25,17},{1,25},{10,2},{18... | collective-permute-start | bytes 138248 | tf_op jit(solution)/shard_map/ppermute | solution.py:25
  73.9 1.5 %fusion.29 = f32[20,10,384]{2,0,1:T(8,128)S(1)} fusion(f32[20,10,1]{2,0,1:T(8,128)S(1)} %slice-done, f32[20,10,383]{2,0,1:T(8,128)S(1)} %slice.204, f32[20,10,384]{2,0,1:T(8,128)S(1)} %fusion.2, f32[20,10,1]{2,0,1:T(8,128)S(1)} %get-tuple-element.20, f32[20,10,383]{2,0,1:T(8,128)S(1)} %get-tuple-element.22, f32[20,10,2]{2,0,1:T(8,128)S(1)} %slice.209, ...), kind=kLoop, calls=%fused_computation.54 | loop fusion | flops 1459200 | bytes 2150400 | tf_op jit(solution)/shard_map/mul | solution.py:71
  75.4 0.2 fusion.79
  75.9 0.2 collective-permute-start.6
  76.2 2.7 %collective-permute-start.7 = (f32[26,3,384]{2,0,1:T(8,128)S(1)}, f32[26,3,384]{2,0,1:T(8,128)S(1)}, u32[]{:S(2)}, u32[]{:S(2)}) collective-permute-start(f32[26,3,384]{2,0,1:T(8,128)S(1)} %get-tuple-element.7), channel_id=1, source_target_pairs={{1,0},{2,1},{3,2},{4,3},{5,4},{6,5},{7,6},{0,7},{9,8},{10,9},{11,1... | collective-permute-start | bytes 359432 | tf_op jit(solution)/shard_map/ppermute | solution.py:25
  78.9 0.2 fusion.26
  79.1 3.8 %collective-permute-done.6 = f32[26,3,384]{2,0,1:T(8,128)S(1)} collective-permute-done((f32[26,3,384]{2,0,1:T(8,128)S(1)}, f32[26,3,384]{2,0,1:T(8,128)S(1)}, u32[]{:S(2)}, u32[]{:S(2)}) %collective-permute-start.6) | collective-permute-done | bytes 119840 | tf_op jit(solution)/shard_map/ppermute | solution.py:22
  82.9 2.5 %collective-permute-done.7 = f32[26,3,384]{2,0,1:T(8,128)S(1)} collective-permute-done((f32[26,3,384]{2,0,1:T(8,128)S(1)}, f32[26,3,384]{2,0,1:T(8,128)S(1)}, u32[]{:S(2)}, u32[]{:S(2)}) %collective-permute-start.7) | collective-permute-done | bytes 119840 | tf_op jit(solution)/shard_map/ppermute | solution.py:25
  85.6 0.3 fusion.12
  85.8 0.7 copy-done.2
  86.6 2.5 %multiply_reduce_fusion = (f32[]{:T(128)}, f32[]{:T(128)}, f32[20,10,384]{2,0,1:T(8,128)S(1)}) fusion(f32[20,10,384]{2,0,1:T(8,128)S(1)} %fusion.2, f32[20,10,384]{2,0,1:T(8,128)S(1)} %copy-done.2, f32[20,10,382]{2,0,1:T(8,128)S(1)} %bitcast.56, f32[20,10,2]{2,0,1:T(8,128)S(1)} %slice.216, f32[20,10,1]{2,0,1:T(8,128)S(1)} %get-tuple-element.16, ...), kind=kLoop, calls=%fused_computation.65 | loop fusion | flops 2611198 | bytes 4915208 | tf_op jit(solution)/shard_map/reduce_sum | solution.py:147
  89.1 42.5 %all-reduce = (f32[]{:T(128)}, f32[]{:T(128)}) all-reduce(f32[]{:T(128)} %get-tuple-element.3, f32[]{:T(128)} %get-tuple-element.2), channel_id=1, replica_groups=mesh['gx'=4,'gy'=8] {'gx','gy'}, use_global_device_ids=true, to_apply=%region_1.2 | all-reduce | flops 2 | bytes 16 | tf_op jit(solution)/shard_map/psum | solution.py:128
  132.9 0.9 multiply_subtract_fusion
  (40 shorter events, 2.0 us)
Async XLA Ops:
  5.9 10.8 %all-to-all-start = ((f32[4,20,10,96]{3,1,2,0:T(8,128)}), f32[4,20,10,96]{3,1,2,0:T(8,128)S(1)}, u32[]{:S(2)}, u32[]{:S(2)}) async-start(f32[4,20,10,96]{3,1,2,0:T(8,128)} %pad_maximum_fusion.2), calls=%async_computation | async-start | bytes 983040 | tf_op jit(solution)/shard_map/all_to_all | solution.py:99
  18.9 15.2 %all-to-all-start.1 = ((f32[8,1,9600]{2,1,0:T(1,128)}), f32[8,1,9600]{2,1,0:T(1,128)S(1)}, u32[]{:S(2)}, u32[]{:S(2)}) async-start(f32[8,1,9600]{2,1,0:T(1,128)} %reshape.80), calls=%async_computation.1 | async-start | bytes 614400 | tf_op jit(solution)/shard_map/all_to_all | solution.py:105
  39.2 4.7 %copy-start.1 = (f32[20,10,384]{2,0,1:T(8,128)S(1)}, f32[20,10,384]{2,0,1:T(8,128)}, u32[]{:S(2)}) copy-start(f32[20,10,384]{2,0,1:T(8,128)} %param.2) | copy-start | bytes 921604
  39.2 13.2 %all-to-all-start.2 = ((f32[8,1,9600]{2,1,0:T(1,128)}), f32[8,1,9600]{2,1,0:T(1,128)S(1)}, u32[]{:S(2)}, u32[]{:S(2)}) async-start(f32[8,1,9600]{2,1,0:T(1,128)} %reshape.82), calls=%async_computation.2 | async-start | bytes 614400 | tf_op jit(solution)/shard_map/all_to_all | solution.py:121
  45.3 16.0 %copy-start = (f32[20,10,384]{2,0,1:T(8,128)}, f32[20,10,384]{2,0,1:T(8,128)S(1)}, u32[]{:S(2)}) copy-start(f32[20,10,384]{2,0,1:T(8,128)S(1)} %multiply_exponential_fusion) | copy-start | bytes 921604
  45.3 3.4 %collective-permute-start = (f32[2,10,384]{2,0,1:T(2,128)S(1)}, f32[2,10,384]{2,0,1:T(2,128)S(1)}, u32[]{:S(2)}, u32[]{:S(2)}) collective-permute-start(f32[2,10,384]{2,0,1:T(2,128)S(1)} %get-tuple-element.11), channel_id=1, source_target_pairs={{0,8},{8,16},{16,24},{24,0},{1,9},{9,17},{17,25},{25,1},{2,10},{10... | collective-permute-start | bytes 92168 | tf_op jit(solution)/shard_map/ppermute | solution.py:22
  45.4 3.3 %collective-permute-start.1 = (f32[2,10,384]{2,0,1:T(2,128)S(1)}, f32[2,10,384]{2,0,1:T(2,128)S(1)}, u32[]{:S(2)}, u32[]{:S(2)}) collective-permute-start(f32[2,10,384]{2,0,1:T(2,128)S(1)} %get-tuple-element.12), channel_id=1, source_target_pairs={{8,0},{16,8},{24,16},{0,24},{9,1},{17,9},{25,17},{1,25},{10,2},{18... | collective-permute-start | bytes 92168 | tf_op jit(solution)/shard_map/ppermute | solution.py:25
  48.7 12.5 %collective-permute-start.4 = (f32[24,2,384]{2,0,1:T(8,128)S(1)}, f32[24,2,384]{2,0,1:T(8,128)S(1)}, u32[]{:S(2)}, u32[]{:S(2)}) collective-permute-start(f32[24,2,384]{2,0,1:T(8,128)S(1)} %get-tuple-element.9), channel_id=1, source_target_pairs={{0,1},{1,2},{2,3},{3,4},{4,5},{5,6},{6,7},{7,0},{8,9},{9,10},{10,1... | collective-permute-start | bytes 221192 | tf_op jit(solution)/shard_map/ppermute | solution.py:22
  50.2 11.0 %collective-permute-start.5 = (f32[24,2,384]{2,0,1:T(8,128)S(1)}, f32[24,2,384]{2,0,1:T(8,128)S(1)}, u32[]{:S(2)}, u32[]{:S(2)}) collective-permute-start(f32[24,2,384]{2,0,1:T(8,128)S(1)} %get-tuple-element.10), channel_id=1, source_target_pairs={{1,0},{2,1},{3,2},{4,3},{5,4},{6,5},{7,6},{0,7},{9,8},{10,9},{11,1... | collective-permute-start | bytes 221192 | tf_op jit(solution)/shard_map/ppermute | solution.py:25
  56.3 9.7 %all-to-all-start.3 = ((f32[4,1,19200]{2,1,0:T(1,128)}), f32[4,1,19200]{2,1,0:T(1,128)S(1)}, u32[]{:S(2)}, u32[]{:S(2)}) async-start(f32[4,1,19200]{2,1,0:T(1,128)} %reshape.84), calls=%async_computation.3 | async-start | bytes 614400 | tf_op jit(solution)/shard_map/all_to_all | solution.py:123
  72.0 1.8 %slice-start = ((f32[20,10,384]{2,0,1:T(8,128)}), f32[20,10,1]{2,0,1:T(8,128)S(1)}, s32[]{:S(2)}) async-start(f32[20,10,384]{2,0,1:T(8,128)} %copy-done), calls=%async_computation.4 | async-start | bytes 245760 | tf_op jit(solution)/shard_map/jit(_roll_static)/slice | solution.py:141
  72.1 3.7 %collective-permute-start.2 = (f32[3,10,384]{2,0,1:T(4,128)S(1)}, f32[3,10,384]{2,0,1:T(4,128)S(1)}, u32[]{:S(2)}, u32[]{:S(2)}) collective-permute-start(f32[3,10,384]{2,0,1:T(4,128)S(1)} %get-tuple-element.13), channel_id=1, source_target_pairs={{0,8},{8,16},{16,24},{24,0},{1,9},{9,17},{17,25},{25,1},{2,10},{10... | collective-permute-start | bytes 138248 | tf_op jit(solution)/shard_map/ppermute | solution.py:22
  72.1 3.7 %collective-permute-start.3 = (f32[3,10,384]{2,0,1:T(4,128)S(1)}, f32[3,10,384]{2,0,1:T(4,128)S(1)}, u32[]{:S(2)}, u32[]{:S(2)}) collective-permute-start(f32[3,10,384]{2,0,1:T(4,128)S(1)} %get-tuple-element.14), channel_id=1, source_target_pairs={{8,0},{16,8},{24,16},{0,24},{9,1},{17,9},{25,17},{1,25},{10,2},{18... | collective-permute-start | bytes 138248 | tf_op jit(solution)/shard_map/ppermute | solution.py:25
  75.9 7.0 %collective-permute-start.6 = (f32[26,3,384]{2,0,1:T(8,128)S(1)}, f32[26,3,384]{2,0,1:T(8,128)S(1)}, u32[]{:S(2)}, u32[]{:S(2)}) collective-permute-start(f32[26,3,384]{2,0,1:T(8,128)S(1)} %get-tuple-element.8), channel_id=1, source_target_pairs={{0,1},{1,2},{2,3},{3,4},{4,5},{5,6},{6,7},{7,0},{8,9},{9,10},{10,1... | collective-permute-start | bytes 359432 | tf_op jit(solution)/shard_map/ppermute | solution.py:22
  76.2 9.3 %collective-permute-start.7 = (f32[26,3,384]{2,0,1:T(8,128)S(1)}, f32[26,3,384]{2,0,1:T(8,128)S(1)}, u32[]{:S(2)}, u32[]{:S(2)}) collective-permute-start(f32[26,3,384]{2,0,1:T(8,128)S(1)} %get-tuple-element.7), channel_id=1, source_target_pairs={{1,0},{2,1},{3,2},{4,3},{5,4},{6,5},{7,6},{0,7},{9,8},{10,9},{11,1... | collective-permute-start | bytes 359432 | tf_op jit(solution)/shard_map/ppermute | solution.py:25
  85.6 1.0 copy-start.2
